TPU v7x, 32 devices: a whole 2x2x4 slice. The times are simulated.
32 devices in a mesh: fsdp: 2 (over y), ctx: 4 (over x, core), tp: 4 (over z).
Axes of the slice: x: 2, y: 2, z: 4, core: 2. Of those that a mesh axis runs over, the one named last changes fastest.
Arguments:
- tokens: bfloat16 [12608, 512], P(('fsdp', 'ctx', 'tp')), may hold values from -6 to 6
- w_qkv: float32 [512, 1536], P(('fsdp', 'ctx', 'tp')), may hold values from -0.375 to 0.375
- w_attend: float32 [512, 512], P(('fsdp', 'ctx', 'tp')), may hold values from -0.75 to 0.75
- w_route: float32 [512, 8], P(('fsdp', 'ctx', 'tp')), may hold values from -0.1875 to 0.1875
- gain_one: float32 [512], P(('fsdp', 'ctx', 'tp')), may hold values from 0.5 to 1.5
- shift_one: float32 [512], P(('fsdp', 'ctx', 'tp')), may hold values from -1 to 1
- gain_two: float32 [512], P(('fsdp', 'ctx', 'tp')), may hold values from 0.5 to 1.5
- shift_two: float32 [512], P(('fsdp', 'ctx', 'tp')), may hold values from -1 to 1
- w_up: float32 [8, 512, 2048], P(None, ('fsdp', 'ctx'), 'tp'), may hold values from -0.25 to 0.25
- w_down: float32 [8, 512, 2048], P(None, ('fsdp', 'ctx'), 'tp'), may hold values from -0.75 to 0.75
- routes: int32 [12608, 2], P(('fsdp', 'ctx')), may hold values from 0 to 7, all different within a row
- priority: int32 [8, 1576], P(('fsdp', 'ctx')), may hold values from 0 to 1575, each once within a row
- cotangent: bfloat16 [12608, 512], P(('fsdp', 'ctx', 'tp')), may hold values from -6 to 6
Outputs:
- output: bfloat16 [12608, 512], P(('fsdp', 'ctx', 'tp'))
- grad_tokens: bfloat16 [12608, 512], P(('fsdp', 'ctx', 'tp'))
- grad_qkv: float32 [512, 1536], P(('fsdp', 'ctx', 'tp'))
- grad_attend: float32 [512, 512], P(('fsdp', 'ctx', 'tp'))
- grad_route: float32 [512, 8], P(('fsdp', 'ctx', 'tp'))
- grad_gain_one: float32 [512], P(('fsdp', 'ctx', 'tp'))
- grad_shift_one: float32 [512], P(('fsdp', 'ctx', 'tp'))
- grad_gain_two: float32 [512], P(('fsdp', 'ctx', 'tp'))
- grad_shift_two: float32 [512], P(('fsdp', 'ctx', 'tp'))
- grad_up: float32 [8, 512, 2048], P(None, ('fsdp', 'ctx'), 'tp')
- grad_down: float32 [8, 512, 2048], P(None, ('fsdp', 'ctx'), 'tp')
Inputs may be any that keep to these rules, and one draw needn't show every extreme that they name: `routes`: each row names 2 different experts, and every expert is named by some row. `priority`: each row is a permutation of 0 to 1575.
All inputs are finite; a program needn't handle non-finite values.
Results may differ from a plain program's by a relative error of at most 0.015.
The roundings to bfloat16 on the way count: a program that leaves them out, or rounds other values in their place, can miss the bound.
Values may be sent and summed in bfloat16 or wider, within the bound.
No kernel may reach another device: no remote copies, remote signals or barrier semaphores. Data moves between devices by JAX's collectives and lax.ppermute only.
A program may use at most 192 MiB of HBM per device.

v0:
```python
from functools import partial
import math
import jax
import jax.numpy as jnp
from jax import lax
from jax.sharding import PartitionSpec as P

D = 512
HEADS = 8
HEAD = 64
SEQ = 197
TOP = 2
EXPERTS = 8
epsilon = 1e-06


def norm_forward(values):
    center = values - jnp.mean(values, axis=-1, keepdims=True)
    spread = jnp.mean(center * center, axis=-1, keepdims=True)
    inv_scale = lax.rsqrt(spread + epsilon)
    return (center * inv_scale, inv_scale)


def norm_backward(grad_norm, normed, inv_scale, gain_row):
    scaled = grad_norm * gain_row
    centred = scaled - jnp.mean(scaled, axis=-1, keepdims=True)
    return inv_scale * (centred - normed * jnp.mean(scaled * normed, axis=-1, keepdims=True))


def rows_product(left, right):
    return lax.dot_general(
        left, right, (((0,), (0,)), ((), ())), preferred_element_type=jnp.float32
    )


def times_transpose(left, right):
    return lax.dot_general(
        left, right, (((1,), (1,)), ((), ())), preferred_element_type=jnp.float32
    )


def slot_tables(routes_group, order_group, capacity):
    row_count = order_group.shape[0]
    inverse = (
        jnp.zeros((row_count,), jnp.int32)
        .at[order_group]
        .set(jnp.arange(row_count, dtype=jnp.int32))
    )
    ordered = routes_group[inverse].T.reshape(-1)
    expert_ids = jnp.arange(EXPERTS, dtype=jnp.int32)
    onehot = (ordered[:, None] == expert_ids[None, :]).astype(jnp.int32)
    earlier = jnp.cumsum(onehot, axis=0) - onehot
    slot_keyed = jnp.sum(earlier * onehot, axis=1).reshape(TOP, row_count)
    slot_index = slot_keyed[:, order_group].T
    kept_pair = slot_index < capacity
    position = jnp.where(kept_pair, routes_group * capacity + slot_index, 0)
    target = jnp.where(kept_pair, position, EXPERTS * capacity).reshape(-1)
    owners = jnp.broadcast_to(
        jnp.arange(row_count, dtype=jnp.int32)[:, None], (row_count, TOP)
    ).reshape(-1)
    slot_table = (
        jnp.full((EXPERTS * capacity,), row_count, jnp.int32).at[target].set(owners, mode="drop")
    )
    return (kept_pair, position, slot_table, target)


def fetch_experts(w_up, w_down):
    whole = (
        lax.all_gather(w_up.astype(jnp.bfloat16), ("fsdp", "ctx"), axis=1, tiled=True),
        lax.all_gather(w_down.astype(jnp.bfloat16), ("fsdp", "ctx"), axis=1, tiled=True),
    )
    return (whole[0], whole[1])


def on_device(
    tokens,
    w_qkv,
    w_attend,
    w_route,
    gain_one,
    shift_one,
    gain_two,
    shift_two,
    w_up,
    w_down,
    routes,
    priority,
    cotangent,
):
    tok_rows = tokens.shape[0]
    ctx_size = lax.axis_size("ctx")
    tp_size = lax.axis_size("tp")
    images = tok_rows // SEQ
    head_width = D // ctx_size
    local_heads = HEADS // ctx_size
    score_scale = 1.0 / math.sqrt(HEAD)
    group_rows = tok_rows * tp_size
    capacity = group_rows * TOP * 5 // (4 * EXPERTS)
    gathered = (
        lax.all_gather(w_qkv.astype(jnp.bfloat16), ("fsdp", "ctx", "tp"), axis=0, tiled=True),
        lax.all_gather(w_attend.astype(jnp.bfloat16), ("fsdp", "ctx", "tp"), axis=0, tiled=True),
        lax.all_gather(w_route.astype(jnp.bfloat16), ("fsdp", "ctx", "tp"), axis=0, tiled=True),
        lax.all_gather(gain_one.astype(jnp.bfloat16), ("fsdp", "ctx", "tp"), axis=0, tiled=True),
        lax.all_gather(shift_one.astype(jnp.bfloat16), ("fsdp", "ctx", "tp"), axis=0, tiled=True),
        lax.all_gather(gain_two.astype(jnp.bfloat16), ("fsdp", "ctx", "tp"), axis=0, tiled=True),
        lax.all_gather(shift_two.astype(jnp.bfloat16), ("fsdp", "ctx", "tp"), axis=0, tiled=True),
    )
    qkv_w = gathered[0]
    attend_w = gathered[1]
    route_w = gathered[2]
    gain_a = gathered[3].astype(jnp.float32)
    offset_a = gathered[4].astype(jnp.float32)
    gain_b = gathered[5].astype(jnp.float32)
    offset_b = gathered[6].astype(jnp.float32)
    inputs_f = tokens.astype(jnp.float32)
    normed_one, inv_one = norm_forward(inputs_f)
    a_one = (normed_one * gain_a + offset_a).astype(jnp.bfloat16)
    projected = jnp.dot(a_one, qkv_w, preferred_element_type=jnp.float32).astype(jnp.bfloat16)
    heads_local = projected.reshape(images, SEQ, 3, ctx_size, head_width)
    by_head = lax.all_to_all(heads_local, "ctx", split_axis=3, concat_axis=0, tiled=True)
    batch_images = by_head.shape[0]
    queries = by_head[:, :, 0, 0].reshape(batch_images, SEQ, local_heads, HEAD)
    keys_all = by_head[:, :, 1, 0].reshape(batch_images, SEQ, local_heads, HEAD)
    values_all = by_head[:, :, 2, 0].reshape(batch_images, SEQ, local_heads, HEAD)
    scores = (
        jnp.einsum("bqhd,bkhd->bhqk", queries, keys_all, preferred_element_type=jnp.float32)
        * score_scale
    )
    row_peak = jnp.max(scores, axis=-1, keepdims=True)
    log_total = row_peak + jnp.log(jnp.sum(jnp.exp(scores - row_peak), axis=-1, keepdims=True))
    weights_low = jnp.exp(scores - log_total).astype(jnp.bfloat16)
    context_heads = jnp.einsum(
        "bhqk,bkhd->bqhd", weights_low, values_all, preferred_element_type=jnp.float32
    ).astype(jnp.bfloat16)
    back_rows = lax.all_to_all(
        context_heads.reshape(batch_images, SEQ, 1, head_width),
        "ctx",
        split_axis=0,
        concat_axis=2,
        tiled=True,
    )
    context = back_rows.reshape(tok_rows, D)
    y_one = inputs_f + jnp.dot(context, attend_w, preferred_element_type=jnp.float32)
    normed_two, inv_two = norm_forward(y_one)
    a_two = (normed_two * gain_b + offset_b).astype(jnp.bfloat16)
    a_group, cot_group = (
        lax.all_gather(a_two, "tp", axis=0, tiled=True),
        lax.all_gather(cotangent, "tp", axis=0, tiled=True),
    )
    logits = jnp.dot(a_group, route_w, preferred_element_type=jnp.float32)
    gate_probs = jax.nn.softmax(logits, axis=-1)
    kept_pair, position, slot_table, flat_target = slot_tables(routes, priority[0], capacity)
    expert_ids = jnp.arange(EXPERTS, dtype=jnp.int32)
    route_onehot = (routes[:, :, None] == expert_ids[None, None, :]).astype(jnp.float32)
    weight_pair = jnp.where(kept_pair, jnp.sum(gate_probs[:, None, :] * route_onehot, axis=-1), 0.0)
    slot_gate = (
        jnp.zeros((EXPERTS * capacity,), jnp.float32)
        .at[flat_target]
        .set(weight_pair.reshape(-1), mode="drop")
    )
    local_count = EXPERTS
    pair_float = kept_pair.astype(jnp.float32)
    padded = jnp.concatenate([a_group, jnp.zeros((1, D), jnp.bfloat16)], axis=0)
    expert_in = padded[slot_table].reshape(local_count, capacity, D)
    up_w, down_w = fetch_experts(w_up, w_down)
    pre_act = jnp.einsum("ecd,edf->ecf", expert_in, up_w, preferred_element_type=jnp.float32)
    hidden = jax.nn.gelu(pre_act, approximate=True).astype(jnp.bfloat16)
    expert_out = jnp.einsum(
        "ecf,edf->ecd", hidden, down_w, preferred_element_type=jnp.float32
    ).reshape(local_count * capacity, D)
    picked = expert_out[position] * pair_float[:, :, None]
    combined = jnp.sum(picked * weight_pair[:, :, None], axis=1)
    moe_rows = lax.psum_scatter(
        combined.astype(jnp.bfloat16), "tp", scatter_dimension=0, tiled=True
    ).astype(jnp.float32)
    output = (y_one + moe_rows).astype(jnp.bfloat16)
    cot_float = cot_group.astype(jnp.float32)
    grad_weight = jnp.where(kept_pair, jnp.einsum("gjd,gd->gj", picked, cot_float), 0.0)
    cot_padded = jnp.concatenate([cot_group, jnp.zeros((1, D), jnp.bfloat16)], axis=0)
    grad_out = (
        (cot_padded[slot_table].astype(jnp.float32) * slot_gate[:, None])
        .astype(jnp.bfloat16)
        .reshape(local_count, capacity, D)
    )
    up_back, down_back = fetch_experts(w_up, w_down)
    grad_hidden = jnp.einsum(
        "ecd,edf->ecf", grad_out, down_back, preferred_element_type=jnp.float32
    )
    gelu_pull = jax.vjp(partial(jax.nn.gelu, approximate=True), pre_act)[1]
    grad_pre = gelu_pull(grad_hidden)[0].astype(jnp.bfloat16)
    grad_down_full = jnp.einsum(
        "ecd,ecf->edf", grad_out, hidden, preferred_element_type=jnp.float32
    )
    grad_up_full = jnp.einsum(
        "ecd,ecf->edf", expert_in, grad_pre, preferred_element_type=jnp.float32
    )
    grad_in = jnp.einsum(
        "ecf,edf->ecd", grad_pre, up_back, preferred_element_type=jnp.float32
    ).reshape(local_count * capacity, D)
    grad_group = jnp.sum(grad_in[position] * pair_float[:, :, None], axis=1)
    grad_moe, grad_weight_own = (
        lax.psum_scatter(grad_group, "tp", scatter_dimension=0, tiled=True),
        lax.psum_scatter(grad_weight, "tp", scatter_dimension=0, tiled=True),
    )
    start_row = lax.axis_index("tp") * tok_rows
    gates_own = lax.dynamic_slice_in_dim(gate_probs, start_row, tok_rows, 0)
    onehot_own = lax.dynamic_slice_in_dim(route_onehot, start_row, tok_rows, 0)
    grad_gates = jnp.sum(grad_weight_own[:, :, None] * onehot_own, axis=1)
    grad_logits = (
        gates_own * (grad_gates - jnp.sum(gates_own * grad_gates, axis=-1, keepdims=True))
    ).astype(jnp.bfloat16)
    grad_route_full = rows_product(a_two, grad_logits)
    grad_a_two = grad_moe + times_transpose(grad_logits, route_w)
    grad_gain_b = jnp.sum(grad_a_two * normed_two, axis=0)
    grad_offset_b = jnp.sum(grad_a_two, axis=0)
    grad_y_one = cotangent.astype(jnp.float32) + norm_backward(
        grad_a_two, normed_two, inv_two, gain_b
    )
    grad_branch = grad_y_one.astype(jnp.bfloat16)
    grad_attend_full = rows_product(context, grad_branch)
    grad_context = times_transpose(grad_branch, attend_w).astype(jnp.bfloat16)
    grad_heads = lax.all_to_all(
        grad_context.reshape(images, SEQ, ctx_size, head_width),
        "ctx",
        split_axis=2,
        concat_axis=0,
        tiled=True,
    )
    grad_heads = grad_heads.reshape(batch_images, SEQ, local_heads, HEAD)
    scores_again = (
        jnp.einsum("bqhd,bkhd->bhqk", queries, keys_all, preferred_element_type=jnp.float32)
        * score_scale
    )
    weights_again = jnp.exp(scores_again - log_total)
    grad_weights = jnp.einsum(
        "bqhd,bkhd->bhqk", grad_heads, values_all, preferred_element_type=jnp.float32
    )
    grad_values = jnp.einsum(
        "bhqk,bqhd->bkhd",
        weights_again.astype(jnp.bfloat16),
        grad_heads,
        preferred_element_type=jnp.float32,
    )
    row_dot = jnp.sum(weights_again * grad_weights, axis=-1, keepdims=True)
    grad_scores = (weights_again * (grad_weights - row_dot)).astype(jnp.bfloat16)
    grad_queries = (
        jnp.einsum("bhqk,bkhd->bqhd", grad_scores, keys_all, preferred_element_type=jnp.float32)
        * score_scale
    )
    grad_keys = (
        jnp.einsum("bhqk,bqhd->bkhd", grad_scores, queries, preferred_element_type=jnp.float32)
        * score_scale
    )
    grad_proj = jnp.stack([grad_queries, grad_keys, grad_values], axis=2).astype(jnp.bfloat16)
    grad_proj = grad_proj.reshape(batch_images, SEQ, 3, 1, head_width)
    grad_rows = lax.all_to_all(grad_proj, "ctx", split_axis=0, concat_axis=3, tiled=True).reshape(
        tok_rows, 3 * D
    )
    grad_qkv_full = rows_product(a_one, grad_rows)
    grad_a_one = times_transpose(grad_rows, qkv_w)
    grad_gain_a = jnp.sum(grad_a_one * normed_one, axis=0)
    grad_offset_a = jnp.sum(grad_a_one, axis=0)
    grad_tokens = (grad_y_one + norm_backward(grad_a_one, normed_one, inv_one, gain_a)).astype(
        jnp.bfloat16
    )
    summed = (
        lax.psum_scatter(grad_qkv_full, ("fsdp", "ctx", "tp"), scatter_dimension=0, tiled=True),
        lax.psum_scatter(grad_attend_full, ("fsdp", "ctx", "tp"), scatter_dimension=0, tiled=True),
        lax.psum_scatter(grad_route_full, ("fsdp", "ctx", "tp"), scatter_dimension=0, tiled=True),
        lax.psum_scatter(grad_gain_a, ("fsdp", "ctx", "tp"), scatter_dimension=0, tiled=True),
        lax.psum_scatter(grad_offset_a, ("fsdp", "ctx", "tp"), scatter_dimension=0, tiled=True),
        lax.psum_scatter(grad_gain_b, ("fsdp", "ctx", "tp"), scatter_dimension=0, tiled=True),
        lax.psum_scatter(grad_offset_b, ("fsdp", "ctx", "tp"), scatter_dimension=0, tiled=True),
    )
    grad_up_part, grad_down_part = (
        lax.psum_scatter(grad_up_full, ("fsdp", "ctx"), scatter_dimension=1, tiled=True),
        lax.psum_scatter(grad_down_full, ("fsdp", "ctx"), scatter_dimension=1, tiled=True),
    )
    return (
        output,
        grad_tokens,
        summed[0],
        summed[1],
        summed[2],
        summed[3],
        summed[4],
        summed[5],
        summed[6],
        grad_up_part,
        grad_down_part,
    )


def solution(mesh):
    in_specs = (
        P(("fsdp", "ctx", "tp"), None),
        P(("fsdp", "ctx", "tp"), None),
        P(("fsdp", "ctx", "tp"), None),
        P(("fsdp", "ctx", "tp"), None),
        P(("fsdp", "ctx", "tp")),
        P(("fsdp", "ctx", "tp")),
        P(("fsdp", "ctx", "tp")),
        P(("fsdp", "ctx", "tp")),
        P(None, ("fsdp", "ctx"), "tp"),
        P(None, ("fsdp", "ctx"), "tp"),
        P(("fsdp", "ctx"), None),
        P(("fsdp", "ctx"), None),
        P(("fsdp", "ctx", "tp"), None),
    )
    out_specs = (
        P(("fsdp", "ctx", "tp"), None),
        P(("fsdp", "ctx", "tp"), None),
        P(("fsdp", "ctx", "tp"), None),
        P(("fsdp", "ctx", "tp"), None),
        P(("fsdp", "ctx", "tp"), None),
        P(("fsdp", "ctx", "tp")),
        P(("fsdp", "ctx", "tp")),
        P(("fsdp", "ctx", "tp")),
        P(("fsdp", "ctx", "tp")),
        P(None, ("fsdp", "ctx"), "tp"),
        P(None, ("fsdp", "ctx"), "tp"),
    )
    return jax.shard_map(
        on_device, mesh=mesh, in_specs=in_specs, out_specs=out_specs, check_vma=False
    )
```

profile of v0, /device:TPU:0, one launch (start us, length us, event | category | flops | bytes accessed | tf_op | source)
XLA Modules:
  0.0 1153.1 jit_solution(11126072074795200958)
XLA Ops:
  13.1 42.1 %all-reduce.18 = (bf16[512]{0:T(512)(128)(2,1)S(1)}, bf16[512]{0:T(512)(128)(2,1)S(1)}, bf16[512]{0:T(512)(128)(2,1)S(1)}, bf16[512]{0:T(512)(128)(2,1)S(1)}) all-reduce(bf16[512]{0:T(512)(128)(2,1)S(1)} %dynamic-update-slice.1, bf16[512]{0:T(512)(128)(2,1)S(1)} %dynamic-update-slice, ...), channel_id=1, replica_groups=mesh['fsdp'=2,'ctx'=4,'tp'=4] {'fsdp','ctx','tp'}, use_global_device_ids=true, to_apply=%add.4 | all-reduce | flops 2048 | bytes 8192
  57.7 12.3 %all-gather.9.cloned.1.call-done = bf16[512,1536]{1,0:T(8,128)(2,1)} async-done(((bf16[16,1536]{1,0:T(8,128)(2,1)}), bf16[512,1536]{1,0:T(8,128)(2,1)}) %all-gather.9.cloned.1.call-update) | async-done | bytes 1572880 | tf_op jit(solution)/shard_map/all_gather | solution.py:100
  70.0 2.4 convolution_convert_fusion
  72.9 2.0 copy.128
  74.9 3.5 all-to-all-start
  79.0 15.6 %all-to-all-done = bf16[2,197,3,4,128]{4,0,2,1,3:T(2,128)(2,1)S(1)} async-done(((bf16[2,197,3,4,128]{4,0,2,1,3:T(2,128)(2,1)}), bf16[2,197,3,4,128]{4,0,2,1,3:T(2,128)(2,1)S(1)}, u32[]{:S(2)}, u32[]{:S(2)}) %all-to-all-start) | async-done | bytes 1210400 | tf_op jit(solution)/shard_map/all_to_all | solution.py:120
  99.4 2.3 copy.130
  103.0 2.6 convolution_convert_fusion.2
  105.6 2.0 copy.134
  107.6 3.6 all-to-all-start.1
  111.3 71.7 %all_gather.38 = bf16[512,512]{1,0:T(8,128)(2,1)S(1)} all-gather(bf16[16,512]{1,0:T(8,128)(2,1)S(1)} %convert_element_type.137), channel_id=1, replica_groups=mesh['fsdp'=2,'ctx'=4,'tp'=4] {'fsdp','ctx','tp'}, dimensions={0}, use_global_device_ids=true | all-gather | bytes 540672 | tf_op jit(solution)/shard_map/all_gather | solution.py:101
  189.6 66.0 %all-gather.1 = bf16[32,16,8]{1,2,0:T(8,128)(2,1)S(1)} all-gather(bf16[1,16,8]{1,2,0:T(8,128)(2,1)S(1)} %convert_bitcast_fusion.1), channel_id=1, replica_groups=mesh['fsdp'=2,'ctx'=4,'tp'=4] {'fsdp','ctx','tp'}, dimensions={0}, use_global_device_ids=true | all-gather | bytes 8448 | tf_op jit(solution)/shard_map/all_gather | solution.py:102
  256.1 9.1 scatter_custom_fusion
  265.2 3.2 gather_fusion
  268.8 2.3 reduce-window.6
  272.6 3.2 gather_fusion.1
  278.4 15.8 %scatter_custom_fusion.1 = s32[3936]{0:T(1024)S(1)} fusion(s32[3152]{0:T(1024)S(1)} %fusion.42, s32[3152]{0:T(1024)S(1)} %reshape.330, s32[]{:T(128)} %constant.26.clone.1), kind=kCustom, calls=%fused_computation.109 | custom fusion | bytes 15748 | tf_op jit(solution)/shard_map/scatter | solution.py:62
  298.2 12.3 %gather_fusion.4 = bf16[3936,512]{1,0:T(8,128)(2,1)} fusion(bf16[1577,512]{1,0:T(8,128)(2,1)S(1)} %concatenate.15, s32[4096]{0:T(1024)S(1)} %pad_clamp_fusion.1), kind=kCustom, calls=%fused_computation.4 | custom fusion | bytes 8076672 | tf_op jit(solution)/shard_map/gather | solution.py:181
  310.5 6.1 reshape.269
  316.6 2.6 reshape.366
  323.1 12.4 %gather_fusion.2 = bf16[3936,512]{1,0:T(8,128)(2,1)} fusion(bf16[1577,512]{1,0:T(8,128)(2,1)S(1)} %concatenate.14, s32[4096]{0:T(1024)S(1)} %pad_clamp_fusion.1), kind=kCustom, calls=%fused_computation.2 | custom fusion | bytes 8076672 | tf_op jit(solution)/shard_map/gather | solution.py:164
  335.4 4.9 reshape.261
  340.3 9.0 fusion.61
  349.3 10.5 fusion.55
  359.8 7.1 reshape.262
  366.9 14.1 %gather_fusion.3 = f32[3152,512]{1,0:T(8,128)} fusion(f32[3936,512]{1,0:T(8,128)} %reshape.262, s32[4096]{0:T(1024)S(1)} %pad_clamp_fusion), kind=kCustom, calls=%fused_computation.3 | custom fusion | bytes 12923200 | tf_op jit(solution)/shard_map/gather | solution.py:171
  381.0 8.5 reshape.295
  389.5 20.8 %fusion.10 = f32[1576,1,2]{2,1,0:T(1,128)S(1)} fusion(bf16[1576,512,1]{1,2,0:T(2,128)(2,1)S(1)} %copy-done.15, f32[1576,2,512]{2,1,0:T(2,128)} %reshape.295, f32[1576,2]{1,0:T(8,128)} %get-tuple-element.34), kind=kOutput, calls=%fused_computation.22 | convolution fusion | flops 4841472 | bytes 8094336 | tf_op jit(solution)/shard_map/gjd,gd->gj/dot_general | solution.py:178
  410.9 16.0 %scatter_custom_fusion.2 = f32[3936]{0:T(1024)S(1)} fusion(s32[3152]{0:T(1024)} %copy-done.34, f32[3152]{0:T(1024)S(1)} %reshape.338, f32[]{:T(128)} %constant.20.clone.1), kind=kCustom, calls=%fused_computation.107 | custom fusion | bytes 16256 | tf_op jit(solution)/shard_map/scatter | solution.py:159
  427.0 11.9 %fusion.9 = bf16[8,492,512]{2,1,0:T(8,128)(2,1)S(1)} fusion(f32[8,492,512]{2,1,0:T(8,128)} %fusion.61, bf16[8,512,512]{2,1,0:T(8,128)(2,1)} %all-gather.13.cloned.1.call-done, f32[8,492,512]{2,1,0:T(8,128)} %reshape.269, f32[8,492]{1,0:T(8,128)S(1)} %mul.246), kind=kOutput, calls=%fused_computation.17 | convolution fusion | flops 2107932672 | bytes 24362368 | tf_op jit(solution)/shard_map/ecd,edf->ecf/dot_general | solution.py:186
  439.0 2.0 copy-done.5
  441.0 5.6 fusion.62
  446.5 7.0 reshape.264
  453.5 14.1 %gather_fusion.5 = f32[3152,512]{1,0:T(8,128)} fusion(f32[3936,512]{1,0:T(8,128)} %reshape.264, s32[4096]{0:T(1024)S(1)} %pad_clamp_fusion), kind=kCustom, calls=%fused_computation.5 | custom fusion | bytes 12923200 | tf_op jit(solution)/shard_map/gather | solution.py:200
  467.7 8.3 reshape.311
  476.0 20.3 %multiply_reduce_fusion = (f32[1576,512]{1,0:T(8,128)}, bf16[1576,512]{1,0:T(8,128)(2,1)S(1)}) fusion(f32[1576,2,512]{2,1,0:T(2,128)} %reshape.311, f32[1576,2]{1,0:T(8,128)} %get-tuple-element.34, f32[1576,2]{1,0:T(8,128)S(1)} %get-tuple-element.44, f32[1576,2,512]{2,1,0:T(2,128)} %reshape.295), kind=kLoop, calls=%fused_computation.20 | loop fusion | flops 6455296 | bytes 17777280 | tf_op jit(solution)/shard_map/reduce_sum | solution.py:200
  496.3 29.7 %fusion = bf16[400,512]{1,0:T(8,128)(2,1)S(1)} fusion(bf16[1576,512]{1,0:T(8,128)(2,1)S(1)} %get-tuple-element.20), kind=kCustom, calls=%all-reduce-scatter | all-reduce-scatter fusion | flops 819201 | bytes 2023936
  527.9 66.7 %fusion.56 = (f32[400,2]{1,0:T(8,128)S(1)}, f32[400,512]{1,0:T(8,128)S(1)}) fusion(f32[1576,2]{1,0:T(8,128)S(1)} %get-tuple-element.43, f32[1576,512]{1,0:T(8,128)} %get-tuple-element.19), kind=kCustom, calls=%all-reduce-scatter.3 | all-reduce-scatter fusion | flops 822401 | bytes 4063168
  596.0 3.6 collective-permute-start.1
  602.8 2.0 concatenate.17
  605.5 2.1 multiply_add_fusion
  609.7 2.0 reshape.265
  611.8 2.1 copy.145
  613.8 4.1 all-to-all-start.2
  618.0 2.4 fusion.63
  620.4 2.7 fusion.35
  623.2 2.3 all-to-all-done.2
  625.5 2.0 copy.146
  627.5 2.2 multiply_reduce_fusion.2
  633.0 2.0 copy.150
  635.0 3.0 fusion.17
  638.0 2.0 copy.151
  640.0 2.6 convolution_convert_fusion.1
  645.2 19.0 %all_to_all.63 = bf16[8,197,3,1,128]{4,1,2,3,0:T(8,128)(2,1)S(1)} all-to-all(bf16[8,197,3,1,128]{4,1,2,3,0:T(8,128)(2,1)S(1)} %pad_maximum_fusion), channel_id=1, replica_groups=mesh['fsdp'=2,'ctx'=4,'tp'=4] {'ctx'}, dimensions={0} | all-to-all | bytes 2420736 | tf_op jit(solution)/shard_map/all_to_all | solution.py:256
  666.2 4.1 fusion.52
  670.6 13.6 %fusion.14 = f32[8,512,512]{2,1,0:T(8,128)} fusion(f32[8,492,512]{2,1,0:T(8,128)} %reshape.269, f32[8,492]{1,0:T(8,128)S(1)} %copy-done.36, f32[8,492,512]{2,1,0:T(8,128)} %fusion.61), kind=kOutput, calls=%fused_computation.33 | convolution fusion | flops 2085765120 | bytes 24526208 | tf_op jit(solution)/shard_map/ecd,ecf->edf/dot_general | solution.py:191
  684.3 9.2 fusion.64
  693.5 60.9 %reduce-scatter.22.cloned.1.call-done = f32[16,8]{1,0:T(8,128)} async-done(((f32[512,8]{1,0:T(8,128)}), f32[16,8]{1,0:T(8,128)}) %reduce-scatter.22.cloned.1.call-update) | async-done | bytes 528
  755.8 2.5 fusion.31
  758.3 37.2 %all-reduce.17 = (f32[512]{0:T(512)S(1)}, f32[512]{0:T(512)S(1)}, f32[512]{0:T(512)S(1)}, f32[512]{0:T(512)S(1)}) all-reduce(f32[512]{0:T(512)S(1)} %get-tuple-element.13, f32[512]{0:T(512)S(1)} %get-tuple-element.18, f32[512]{0:T(512)S(1)} %get-tuple-element.11, ...), channel_id=8, replica_groups=mesh['fsdp'=2,'ctx'=4,'tp'=4] {'fsdp','ctx','tp'}, use_global_device_ids=true, to_apply=%region_31.32.clone | all-reduce | flops 2048 | bytes 16384
  798.8 91.7 %reduce-scatter.16.cloned.1.call-done = f32[16,512]{1,0:T(8,128)} async-done(((f32[512,512]{1,0:T(8,128)}), f32[16,512]{1,0:T(8,128)}) %reduce-scatter.16.cloned.1.call-update) | async-done | bytes 32784 | tf_op jit(solution)/shard_map/reduce_scatter | solution.py:268
  890.5 104.8 %reduce-scatter.14.cloned.1.call-done = f32[16,1536]{1,0:T(8,128)} async-done(((f32[512,1536]{1,0:T(8,128)}), f32[16,1536]{1,0:T(8,128)}) %reduce-scatter.14.cloned.1.call-update) | async-done | bytes 98320 | tf_op jit(solution)/shard_map/reduce_scatter | solution.py:267
  995.4 74.3 %reduce-scatter.20.cloned.1.call-done = f32[8,64,512]{2,1,0:T(8,128)} async-done(((f32[8,512,512]{2,1,0:T(8,128)}), f32[8,64,512]{2,1,0:T(8,128)}) %reduce-scatter.20.cloned.1.call-update) | async-done | bytes 1048592 | tf_op jit(solution)/shard_map/reduce_scatter | solution.py:277
  1069.7 75.3 %reduce-scatter.18.cloned.1.call-done = f32[8,64,512]{2,1,0:T(8,128)} async-done(((f32[8,512,512]{2,1,0:T(8,128)}), f32[8,64,512]{2,1,0:T(8,128)}) %reduce-scatter.18.cloned.1.call-update) | async-done | bytes 1048592 | tf_op jit(solution)/shard_map/reduce_scatter | solution.py:276
  (239 shorter events, 56.0 us)
Async XLA Ops:
  8.0 62.0 %all-gather.9.cloned.1.call-start = ((), (), s32[]{:S(2)}) async-start(), calls=%async_computation.9 | async-start | bytes 1622016 | tf_op jit(solution)/shard_map/all_gather | solution.py:100
  55.2 14.9 %copy-start.39 = (f32[512]{0:T(512)}, f32[512]{0:T(512)S(1)}, u32[]{:S(2)}) copy-start(f32[512]{0:T(512)S(1)} %convert_element_type.128) | copy-start | bytes 6148
  55.2 14.9 %copy-start.45 = (f32[512]{0:T(512)}, f32[512]{0:T(512)S(1)}, u32[]{:S(2)}) copy-start(f32[512]{0:T(512)S(1)} %convert_element_type.130) | copy-start | bytes 6148
  56.5 13.6 %copy-start.32 = (f32[394]{0:T(512)}, f32[394]{0:T(512)S(1)}, u32[]{:S(2)}) copy-start(f32[394]{0:T(512)S(1)} %broadcast_multiply_fusion.6) | copy-start | bytes 4732
  57.7 12.3 %copy-start.41 = (f32[394]{0:T(512)}, f32[394]{0:T(512)S(1)}, u32[]{:S(2)}) copy-start(f32[394]{0:T(512)S(1)} %add_rsqrt_fusion.1) | copy-start | bytes 4732
  74.9 19.7 %all-to-all-start = ((bf16[2,197,3,4,128]{4,0,2,1,3:T(2,128)(2,1)}), bf16[2,197,3,4,128]{4,0,2,1,3:T(2,128)(2,1)S(1)}, u32[]{:S(2)}, u32[]{:S(2)}) async-start(bf16[2,197,3,4,128]{4,0,2,1,3:T(2,128)(2,1)} %copy.128), calls=%async_computation | async-start | bytes 2420736 | tf_op jit(solution)/shard_map/all_to_all | solution.py:120
  78.4 217.8 %all-gather.17.cloned.1.call-start = ((), (), s32[]{:S(2)}) async-start(), calls=%async_computation.17 | async-start | bytes 2048000 | tf_op jit(solution)/shard_map/all_gather | solution.py:148
  99.4 6.2 copy-start
  101.8 9.5 copy-start.27
  102.4 0.6 copy-start.22
  107.6 80.1 %copy-start.20 = (f32[8,64,512]{2,1,0:T(8,128)S(1)}, f32[8,64,512]{2,1,0:T(8,128)}, u32[]{:S(2)}) copy-start(f32[8,64,512]{2,1,0:T(8,128)} %param.21) | copy-start | bytes 3145732
  107.6 75.5 %all-to-all-start.1 = ((bf16[8,197,1,128]{3,1,2,0:T(8,128)(2,1)}), bf16[8,197,1,128]{3,1,2,0:T(8,128)(2,1)S(1)}, u32[]{:S(2)}, u32[]{:S(2)}) async-start(bf16[8,197,1,128]{3,1,2,0:T(8,128)(2,1)} %copy.134), calls=%async_computation.1 | async-start | bytes 819200 | tf_op jit(solution)/shard_map/all_to_all | solution.py:135
  111.2 208.0 %all-gather.15.cloned.1.call-start = ((), (), s32[]{:S(2)}) async-start(), calls=%async_computation.16 | async-start | bytes 2048000 | tf_op jit(solution)/shard_map/all_gather | solution.py:147
  111.3 77.3 %copy-start.28 = (f32[512]{0:T(512)}, f32[512]{0:T(512)S(1)}, u32[]{:S(2)}) copy-start(f32[512]{0:T(512)S(1)} %convert_element_type.139) | copy-start | bytes 6148
  111.3 77.3 %copy-start.37 = (f32[512]{0:T(512)}, f32[512]{0:T(512)S(1)}, u32[]{:S(2)}) copy-start(f32[512]{0:T(512)S(1)} %convert_element_type.141) | copy-start | bytes 6148
  183.1 5.5 copy-start.12
  183.2 5.4 copy-start.21
  183.5 0.7 copy-start.14
  184.2 5.3 copy-start.44
  184.2 71.5 %copy-start.24 = (s32[1576,2]{0,1:T(2,128)S(1)}, s32[1576,2]{0,1:T(2,128)}, u32[]{:S(2)}) copy-start(s32[1576,2]{0,1:T(2,128)} %param.23) | copy-start | bytes 37828
  185.8 0.9 copy-start.3
  185.8 70.3 %copy-start.43 = (s32[1,1576]{1,0:T(1,128)S(1)}, s32[1,1576]{1,0:T(1,128)}, u32[]{:S(2)}) copy-start(s32[1,1576]{1,0:T(1,128)} %param.24) | copy-start | bytes 18916
  185.8 69.8 %copy-start.25 = (f32[394]{0:T(512)}, f32[394]{0:T(512)S(1)}, u32[]{:S(2)}) copy-start(f32[394]{0:T(512)S(1)} %broadcast_multiply_fusion.5) | copy-start | bytes 4732
  186.7 68.9 %copy-start.30 = (f32[394]{0:T(512)}, f32[394]{0:T(512)S(1)}, u32[]{:S(2)}) copy-start(f32[394]{0:T(512)S(1)} %add_rsqrt_fusion) | copy-start | bytes 4732
  187.6 152.7 %all-gather.11.cloned.1.call-start = ((), (), s32[]{:S(2)}) async-start(), calls=%async_computation.10 | async-start | bytes 4718592 | tf_op jit(solution)/shard_map/all_gather | solution.py:69
  188.6 160.7 %all-gather.13.cloned.1.call-start = ((), (), s32[]{:S(2)}) async-start(), calls=%async_computation.11 | async-start | bytes 4718592 | tf_op jit(solution)/shard_map/all_gather | solution.py:70
  275.8 18.5 %copy-start.47 = (u32[32]{0:T(128)S(1)}, u32[32]{0:T(128)}, u32[]{:S(2)}) copy-start(u32[32]{0:T(128)} %constant.100) | copy-start | bytes 388
  278.4 32.1 %copy-start.34 = (s32[3152]{0:T(1024)}, s32[3152]{0:T(1024)S(1)}, u32[]{:S(2)}) copy-start(s32[3152]{0:T(1024)S(1)} %fusion.42) | copy-start | bytes 37828
  310.5 6.1 copy-start.9
  381.0 8.5 copy-start.15
  389.5 20.8 %copy-start.16 = (f32[1576,2]{1,0:T(8,128)S(1)}, f32[1576,2]{1,0:T(8,128)}, u32[]{:S(2)}) copy-start(f32[1576,2]{1,0:T(8,128)} %copy.143) | copy-start | bytes 37828
  427.0 11.9 %copy-start.35 = (f32[8,492]{1,0:T(8,128)}, f32[8,492]{1,0:T(8,128)S(1)}, u32[]{:S(2)}) copy-start(f32[8,492]{1,0:T(8,128)S(1)} %mul.246) | copy-start | bytes 47236
  427.0 14.0 %copy-start.2 = (bf16[8,512,512]{2,1,0:T(8,128)(2,1)S(1)}, bf16[8,512,512]{2,1,0:T(8,128)(2,1)}, u32[]{:S(2)}) copy-start(bf16[8,512,512]{2,1,0:T(8,128)(2,1)} %all-gather.11.cloned.1.call-done) | copy-start | bytes 12582916
  438.9 2.0 copy-start.5
  526.0 1.9 copy-start.17
  526.1 75.4 %collective-permute-start = (bf16[18,512]{1,0:T(8,128)(2,1)S(1)}, bf16[18,512]{1,0:T(8,128)(2,1)S(1)}, u32[]{:S(2)}, u32[]{:S(2)}) collective-permute-start(bf16[18,512]{1,0:T(8,128)(2,1)S(1)} %slice.41), channel_id=1, source_target_pairs={{0,1},{1,2},{2,3},{4,5},{5,6},{6,7},{8,9},{9,10},{10,11},{12,13},{... | collective-permute-start | bytes 55304
  527.9 73.6 %copy-start.18 = (bf16[400,512]{1,0:T(8,128)(2,1)S(1)}, bf16[400,512]{1,0:T(8,128)(2,1)}, u32[]{:S(2)}) copy-start(bf16[400,512]{1,0:T(8,128)(2,1)} %copy-done.17) | copy-start | bytes 1228804
  527.9 76.9 %copy-start.4 = (f32[394,512]{1,0:T(8,128)S(1)}, f32[394,512]{1,0:T(8,128)}, u32[]{:S(2)}) copy-start(f32[394,512]{1,0:T(8,128)} %copy-done.3) | copy-start | bytes 2420740
  527.9 76.9 %copy-start.26 = (f32[394]{0:T(512)S(1)}, f32[394]{0:T(512)}, u32[]{:S(2)}) copy-start(f32[394]{0:T(512)} %copy-done.25) | copy-start | bytes 4732
  527.9 76.9 %copy-start.29 = (f32[512]{0:T(512)S(1)}, f32[512]{0:T(512)}, u32[]{:S(2)}) copy-start(f32[512]{0:T(512)} %copy-done.28) | copy-start | bytes 6148
  527.9 76.9 %copy-start.31 = (f32[394]{0:T(512)S(1)}, f32[394]{0:T(512)}, u32[]{:S(2)}) copy-start(f32[394]{0:T(512)} %copy-done.30) | copy-start | bytes 4732
  594.7 4.9 collective-permute-start.2
  596.0 6.8 collective-permute-start.1
  602.7 5.8 copy-start.13
  605.5 12.5 %copy-start.38 = (f32[512]{0:T(512)S(1)}, f32[512]{0:T(512)}, u32[]{:S(2)}) copy-start(f32[512]{0:T(512)} %copy-done.37) | copy-start | bytes 6148
  607.7 0.9 copy-start.7
  609.7 17.8 %copy-start.1 = (f32[8,2,197,197]{2,3,1,0:T(8,128)S(1)}, f32[8,2,197,197]{2,3,1,0:T(8,128)}, u32[]{:S(2)}) copy-start(f32[8,2,197,197]{2,3,1,0:T(8,128)} %copy-done) | copy-start | bytes 7451332
  609.7 17.8 %copy-start.23 = (f32[2,8,197]{2,1,0:T(8,128)S(1)}, f32[2,8,197]{2,1,0:T(8,128)}, u32[]{:S(2)}) copy-start(f32[2,8,197]{2,1,0:T(8,128)} %copy-done.22) | copy-start | bytes 37828
  613.8 11.7 %all-to-all-start.2 = ((bf16[2,197,4,128]{3,0,1,2:T(2,128)(2,1)}), bf16[2,197,4,128]{3,0,1,2:T(2,128)(2,1)}, u32[]{:S(2)}, u32[]{:S(2)}) async-start(bf16[2,197,4,128]{3,0,1,2:T(2,128)(2,1)} %copy.145), calls=%async_computation.2 | async-start | bytes 806912 | tf_op jit(solution)/shard_map/all_to_all | solution.py:222
  618.0 136.4 %reduce-scatter.22.cloned.1.call-start = ((), (), s32[]{:S(2)}) async-start(), calls=%async_computation.18 | async-start | bytes 270336
  620.4 270.2 %reduce-scatter.16.cloned.1.call-start = ((), (), s32[]{:S(2)}) async-start(), calls=%async_computation.13 | async-start | bytes 1081344 | tf_op jit(solution)/shard_map/reduce_scatter | solution.py:268
  623.2 372.2 %reduce-scatter.14.cloned.1.call-start = ((), (), s32[]{:S(2)}) async-start(), calls=%async_computation.12 | async-start | bytes 3244032 | tf_op jit(solution)/shard_map/reduce_scatter | solution.py:267
  629.7 2.0 copy-start.11
  630.6 1.2 copy-start.6
  645.1 21.1 %copy-start.10 = (bf16[394,512]{1,0:T(8,128)(2,1)S(1)}, bf16[394,512]{1,0:T(8,128)(2,1)}, u32[]{:S(2)}) copy-start(bf16[394,512]{1,0:T(8,128)(2,1)} %param.13) | copy-start | bytes 1210372
  645.1 21.1 %copy-start.33 = (f32[394]{0:T(512)S(1)}, f32[394]{0:T(512)}, u32[]{:S(2)}) copy-start(f32[394]{0:T(512)} %copy-done.32) | copy-start | bytes 4732
  645.1 21.0 %copy-start.40 = (f32[512]{0:T(512)S(1)}, f32[512]{0:T(512)}, u32[]{:S(2)}) copy-start(f32[512]{0:T(512)} %copy-done.39) | copy-start | bytes 6148
  645.1 21.0 %copy-start.42 = (f32[394]{0:T(512)S(1)}, f32[394]{0:T(512)}, u32[]{:S(2)}) copy-start(f32[394]{0:T(512)} %copy-done.41) | copy-start | bytes 4732
  645.1 21.0 %copy-start.46 = (f32[512]{0:T(512)S(1)}, f32[512]{0:T(512)}, u32[]{:S(2)}) copy-start(f32[512]{0:T(512)} %copy-done.45) | copy-start | bytes 6148
  666.2 4.4 copy-start.36
  670.3 399.4 %reduce-scatter.20.cloned.1.call-start = ((), (), s32[]{:S(2)}) async-start(), calls=%async_computation.15 | async-start | bytes 9437184 | tf_op jit(solution)/shard_map/reduce_scatter | solution.py:277
  684.2 460.8 %reduce-scatter.18.cloned.1.call-start = ((), (), s32[]{:S(2)}) async-start(), calls=%async_computation.14 | async-start | bytes 9437184 | tf_op jit(solution)/shard_map/reduce_scatter | solution.py:276
  693.5 62.3 %copy-start.19 = (bf16[394,1536]{1,0:T(8,128)(2,1)S(1)}, bf16[394,1536]{1,0:T(8,128)(2,1)}, u32[]{:S(2)}) copy-start(bf16[394,1536]{1,0:T(8,128)(2,1)} %reshape.267) | copy-start | bytes 3631108
  693.5 104.2 %copy-start.8 = (f32[394,512]{1,0:T(8,128)S(1)}, f32[394,512]{1,0:T(8,128)}, u32[]{:S(2)}) copy-start(f32[394,512]{1,0:T(8,128)} %copy-done.7) | copy-start | bytes 2420740
Sparse Core Ops, SparseCore 0:
  12.3 57.6 all-gather.8
  621.0 133.3 reduce-scatter.21
  757.2 133.2 reduce-scatter.15
  896.4 98.9 reduce-scatter.13
  999.3 70.4 reduce-scatter.19
  1073.6 71.3 reduce-scatter.17
Sparse Core Ops, SparseCore 1:
  80.5 39.0 all-gather.16
  187.7 35.3 all-gather.14
  224.9 35.3 all-gather.10
  262.2 36.4 all-gather.12
where the time goes:
time: 1160 us; the launch traced here: 1150 us
  waiting for transfers between devices  438 us (38%)
  blocking collectives  332 us (29%)
  local copies, waits for them, and re-layouts  192 us (17%)
  matrix products  112 us (10%)
  other arithmetic  41.9 us (4%)
  starting transfers between devices  18.6 us (2%)
  between operations  17.9 us (2%)
    unnamed x4, blocking collectives  176 us
    reduce_scatter x1, waiting for transfers between devices, on_device(): lax.psum_scatter(grad_qkv_full, ('fsdp', 'ctx', 'tp'), scatter_dimension=...  105 us
    reduce_scatter x1, waiting for transfers between devices, on_device(): lax.psum_scatter(grad_attend_full, ('fsdp', 'ctx', 'tp'), scatter_dimensi...  91.7 us
    reduce_scatter x1, waiting for transfers between devices, on_device(): lax.psum_scatter(grad_up_full, ('fsdp', 'ctx'), scatter_dimension=1, tile...  75.3 us
    reduce_scatter x1, waiting for transfers between devices, on_device(): lax.psum_scatter(grad_down_full, ('fsdp', 'ctx'), scatter_dimension=1, ti...  74.3 us
    all_gather x1, blocking collectives, on_device(): lax.all_gather(w_attend.astype(jnp.bfloat16), ('fsdp', 'ctx', 'tp'), axis...  71.7 us
    all_gather x1, blocking collectives, on_device(): lax.all_gather(w_route.astype(jnp.bfloat16), ('fsdp', 'ctx', 'tp'), axis=...  66 us
    unnamed x14, waiting for transfers between devices  61.5 us
  transfers between devices with their start and end apart: 16, of which 8 were waited for; matrix products, arithmetic and copies ran while one was open for 21% of the time, Pallas kernels for 0%

commit v1 on v0

--- a/solution.py
+++ b/solution.py
@@ -12,6 +12,18 @@
 TOP = 2
 EXPERTS = 8
 epsilon = 1e-06
+
+
+def gather_by_bits(array, axis, dim):
+    ways, here, hop = (lax.axis_size(axis), lax.axis_index(axis), array.shape[dim])
+    line, have = (array, 1)
+    while have < ways:
+        line = jnp.concatenate(
+            [line, lax.ppermute(line, axis, [(d, (d - have) % ways) for d in range(ways)])],
+            axis=dim,
+        )
+        have = 2 * have
+    return jnp.roll(line, here * hop, axis=dim)
 
 
 def norm_forward(values):
@@ -98,7 +110,7 @@
     capacity = group_rows * TOP * 5 // (4 * EXPERTS)
     gathered = (
         lax.all_gather(w_qkv.astype(jnp.bfloat16), ("fsdp", "ctx", "tp"), axis=0, tiled=True),
-        lax.all_gather(w_attend.astype(jnp.bfloat16), ("fsdp", "ctx", "tp"), axis=0, tiled=True),
+        gather_by_bits(w_attend.astype(jnp.bfloat16), ("fsdp", "ctx", "tp"), 0),
         lax.all_gather(w_route.astype(jnp.bfloat16), ("fsdp", "ctx", "tp"), axis=0, tiled=True),
         lax.all_gather(gain_one.astype(jnp.bfloat16), ("fsdp", "ctx", "tp"), axis=0, tiled=True),
         lax.all_gather(shift_one.astype(jnp.bfloat16), ("fsdp", "ctx", "tp"), axis=0, tiled=True),

time: 1160 us -> 1110 us (0.957)
  blocking collectives: 332 us -> 258 us
  starting transfers between devices: 18.6 us -> 33.2 us
    all_gather x1 -> x0, blocking collectives: 71.7 us -> none  [on_device(): lax.all_gather(w_attend.astype(jnp.bfloat16), ('fsdp', 'ctx', 'tp'), axis...]
    ppermute x0 -> x5, starting transfers between devices: none -> 13.7 us  [gather_by_bits(): lax.ppermute(line, axis, [(d, (d - have) % ways) for d in range(ways)])]
    all_gather x1, waiting for transfers between devices: 12.3 us -> 0.01 us  [on_device(): lax.all_gather(w_qkv.astype(jnp.bfloat16), ('fsdp', 'ctx', 'tp'), axis=0,...]
    unnamed x125 -> x155, local copies, waits for them, and re-layouts: 22.4 us -> 27.6 us
  transfers between devices with their start and end apart: 16 -> 21, of which waited for: 8 -> 11; matrix products, arithmetic and copies ran while one was open for 21% -> 24% of each run, Pallas kernels for 0% -> 0%
where the time goes in v1:
time: 1110 us; the launch traced here: 1090 us
  waiting for transfers between devices  430 us (39%)
  blocking collectives  258 us (23%)
  local copies, waits for them, and re-layouts  199 us (18%)
  matrix products  112 us (10%)
  other arithmetic  44 us (4%)
  starting transfers between devices  33.2 us (3%)
  between operations  18.1 us (2%)
    unnamed x4, blocking collectives  170 us
    reduce_scatter x1, waiting for transfers between devices, on_device(): lax.psum_scatter(grad_qkv_full, ('fsdp', 'ctx', 'tp'), scatter_dimension=...  105 us
    reduce_scatter x1, waiting for transfers between devices, on_device(): lax.psum_scatter(grad_attend_full, ('fsdp', 'ctx', 'tp'), scatter_dimensi...  91.7 us
    reduce_scatter x1, waiting for transfers between devices, on_device(): lax.psum_scatter(grad_up_full, ('fsdp', 'ctx'), scatter_dimension=1, tile...  75.3 us
    reduce_scatter x1, waiting for transfers between devices, on_device(): lax.psum_scatter(grad_down_full, ('fsdp', 'ctx'), scatter_dimension=1, ti...  74.3 us
    all_gather x1, blocking collectives, on_device(): lax.all_gather(w_route.astype(jnp.bfloat16), ('fsdp', 'ctx', 'tp'), axis=...  69.7 us
    unnamed x14, waiting for transfers between devices  62.2 us
    unnamed x155, local copies, waits for them, and re-layouts  27.6 us
  transfers between devices with their start and end apart: 21, of which 11 were waited for; matrix products, arithmetic and copies ran while one was open for 24% of the time, Pallas kernels for 0%

profile of v1, /device:TPU:0, one launch (start us, length us, event | category | flops | bytes accessed | tf_op | source)
XLA Modules:
  0.0 1095.0 jit_solution(273838462007111988)
XLA Ops:
  11.0 6.4 collective-permute-start
  23.3 37.0 %all-reduce.18 = (bf16[512]{0:T(512)(128)(2,1)S(1)}, bf16[512]{0:T(512)(128)(2,1)S(1)}, bf16[512]{0:T(512)(128)(2,1)}, bf16[512]{0:T(512)(128)(2,1)}) all-reduce(bf16[512]{0:T(512)(128)(2,1)S(1)} %dynamic-update-slice.1, bf16[512]{0:T(512)(128)(2,1)S(1)} %dynamic-update-slice, ...), channel_id=1, replica_groups=mesh['fsdp'=2,'ctx'=4,'tp'=4] {'fsdp','ctx','tp'}, use_global_device_ids=true, to_apply=%add.4 | all-reduce | flops 2048 | bytes 8192
  60.4 3.5 collective-permute-start.1
  69.2 2.2 collective-permute-start.3
  71.5 2.4 convolution_convert_fusion
  76.4 3.5 all-to-all-start
  83.2 6.6 collective-permute-done.4
  89.9 6.2 all-to-all-done
  101.0 2.3 copy.130
  104.6 2.6 convolution_convert_fusion.2
  107.2 2.0 copy.134
  109.2 3.5 all-to-all-start.1
  116.6 3.6 all-to-all-done.1
  126.9 69.7 %all-gather.1 = bf16[32,16,8]{1,2,0:T(8,128)(2,1)S(1)} all-gather(bf16[1,16,8]{1,2,0:T(8,128)(2,1)S(1)} %convert_bitcast_fusion.1), channel_id=1, replica_groups=mesh['fsdp'=2,'ctx'=4,'tp'=4] {'fsdp','ctx','tp'}, dimensions={0}, use_global_device_ids=true | all-gather | bytes 8448 | tf_op jit(solution)/shard_map/all_gather | solution.py:114
  197.1 9.1 scatter_custom_fusion
  206.2 3.2 gather_fusion
  209.8 2.3 reduce-window.6
  213.5 3.2 gather_fusion.1
  219.4 15.8 %scatter_custom_fusion.1 = s32[3936]{0:T(1024)S(1)} fusion(s32[3152]{0:T(1024)S(1)} %fusion.44, s32[3152]{0:T(1024)S(1)} %reshape.330, s32[]{:T(128)} %constant.88.clone.1), kind=kCustom, calls=%fused_computation.131 | custom fusion | bytes 15748 | tf_op jit(solution)/shard_map/scatter | solution.py:74
  239.2 12.4 %gather_fusion.4 = bf16[3936,512]{1,0:T(8,128)(2,1)} fusion(bf16[1577,512]{1,0:T(8,128)(2,1)S(1)} %concatenate.42, s32[4096]{0:T(1024)S(1)} %pad_clamp_fusion.1), kind=kCustom, calls=%fused_computation.4 | custom fusion | bytes 8076672 | tf_op jit(solution)/shard_map/gather | solution.py:193
  251.5 6.1 reshape.269
  257.7 2.6 reshape.366
  264.1 12.3 %gather_fusion.2 = bf16[3936,512]{1,0:T(8,128)(2,1)} fusion(bf16[1577,512]{1,0:T(8,128)(2,1)S(1)} %concatenate.41, s32[4096]{0:T(1024)S(1)} %pad_clamp_fusion.1), kind=kCustom, calls=%fused_computation.2 | custom fusion | bytes 8076672 | tf_op jit(solution)/shard_map/gather | solution.py:176
  276.4 4.9 reshape.261
  281.3 8.9 fusion.65
  290.2 10.4 fusion.59
  300.6 7.1 reshape.262
  307.7 14.2 %gather_fusion.3 = f32[3152,512]{1,0:T(8,128)} fusion(f32[3936,512]{1,0:T(8,128)} %reshape.262, s32[4096]{0:T(1024)S(1)} %pad_clamp_fusion), kind=kCustom, calls=%fused_computation.3 | custom fusion | bytes 12923200 | tf_op jit(solution)/shard_map/gather | solution.py:183
  321.9 8.5 reshape.295
  330.4 20.8 %fusion.10 = f32[1576,1,2]{2,1,0:T(1,128)S(1)} fusion(bf16[1576,512,1]{1,2,0:T(2,128)(2,1)S(1)} %copy-done.13, f32[1576,2,512]{2,1,0:T(2,128)} %reshape.295, f32[1576,2]{1,0:T(8,128)} %get-tuple-element.34), kind=kOutput, calls=%fused_computation.22 | convolution fusion | flops 4841472 | bytes 8094336 | tf_op jit(solution)/shard_map/gjd,gd->gj/dot_general | solution.py:190
  351.8 16.0 %scatter_custom_fusion.2 = f32[3936]{0:T(1024)S(1)} fusion(s32[3152]{0:T(1024)} %copy-done.43, f32[3152]{0:T(1024)S(1)} %reshape.338, f32[]{:T(128)} %constant.32.clone.1), kind=kCustom, calls=%fused_computation.129 | custom fusion | bytes 16256 | tf_op jit(solution)/shard_map/scatter | solution.py:171
  367.9 11.9 %fusion.9 = bf16[8,492,512]{2,1,0:T(8,128)(2,1)S(1)} fusion(f32[8,492,512]{2,1,0:T(8,128)} %fusion.65, bf16[8,512,512]{2,1,0:T(8,128)(2,1)} %all-gather.13.cloned.1.call-done, f32[8,492,512]{2,1,0:T(8,128)} %reshape.269, f32[8,492]{1,0:T(8,128)S(1)} %mul.258), kind=kOutput, calls=%fused_computation.17 | convolution fusion | flops 2107932672 | bytes 24362368 | tf_op jit(solution)/shard_map/ecd,edf->ecf/dot_general | solution.py:198
  379.8 2.0 copy-done.5
  381.8 5.5 fusion.66
  387.3 7.0 reshape.264
  394.4 14.1 %gather_fusion.5 = f32[3152,512]{1,0:T(8,128)} fusion(f32[3936,512]{1,0:T(8,128)} %reshape.264, s32[4096]{0:T(1024)S(1)} %pad_clamp_fusion), kind=kCustom, calls=%fused_computation.5 | custom fusion | bytes 12923200 | tf_op jit(solution)/shard_map/gather | solution.py:212
  408.5 8.3 reshape.311
  416.8 20.3 %multiply_reduce_fusion = (f32[1576,512]{1,0:T(8,128)}, bf16[1576,512]{1,0:T(8,128)(2,1)S(1)}) fusion(f32[1576,2,512]{2,1,0:T(2,128)} %reshape.311, f32[1576,2]{1,0:T(8,128)} %get-tuple-element.34, f32[1576,2]{1,0:T(8,128)S(1)} %get-tuple-element.46, f32[1576,2,512]{2,1,0:T(2,128)} %reshape.295), kind=kLoop, calls=%fused_computation.20 | loop fusion | flops 6455296 | bytes 17777280 | tf_op jit(solution)/shard_map/reduce_sum | solution.py:212
  437.2 27.7 %fusion = bf16[400,512]{1,0:T(8,128)(2,1)S(1)} fusion(bf16[1576,512]{1,0:T(8,128)(2,1)S(1)} %get-tuple-element.20), kind=kCustom, calls=%all-reduce-scatter | all-reduce-scatter fusion | flops 819201 | bytes 2023936
  464.9 2.5 collective-permute-start.5
  467.5 67.7 %fusion.60 = (f32[400,2]{1,0:T(8,128)S(1)}, f32[400,512]{1,0:T(8,128)S(1)}) fusion(f32[1576,2]{1,0:T(8,128)S(1)} %get-tuple-element.45, f32[1576,512]{1,0:T(8,128)} %get-tuple-element.19), kind=kCustom, calls=%all-reduce-scatter.3 | all-reduce-scatter fusion | flops 822401 | bytes 4063168
  535.2 2.4 collective-permute-start.7
  537.6 2.9 collective-permute-start.6
  550.3 2.0 reshape.265
  552.3 2.1 copy.145
  554.4 4.1 all-to-all-start.2
  558.5 2.3 fusion.67
  560.9 2.7 fusion.37
  563.7 2.3 all-to-all-done.2
  568.0 2.2 multiply_reduce_fusion.2
  573.5 2.0 copy.150
  575.5 3.0 fusion.17
  580.6 2.5 convolution_convert_fusion.1
  585.7 19.0 %all_to_all.63 = bf16[8,197,3,1,128]{4,1,2,3,0:T(8,128)(2,1)S(1)} all-to-all(bf16[8,197,3,1,128]{4,1,2,3,0:T(8,128)(2,1)S(1)} %pad_maximum_fusion), channel_id=1, replica_groups=mesh['fsdp'=2,'ctx'=4,'tp'=4] {'ctx'}, dimensions={0} | all-to-all | bytes 2420736 | tf_op jit(solution)/shard_map/all_to_all | solution.py:268
  606.8 4.1 fusion.56
  611.2 13.6 %fusion.14 = f32[8,512,512]{2,1,0:T(8,128)} fusion(f32[8,492,512]{2,1,0:T(8,128)} %reshape.269, f32[8,492]{1,0:T(8,128)S(1)} %mul.258, f32[8,492,512]{2,1,0:T(8,128)} %fusion.65), kind=kOutput, calls=%fused_computation.33 | convolution fusion | flops 2085765120 | bytes 24526208 | tf_op jit(solution)/shard_map/ecd,ecf->edf/dot_general | solution.py:203
  624.8 9.2 fusion.68
  634.1 62.0 %reduce-scatter.22.cloned.1.call-done = f32[16,8]{1,0:T(8,128)} async-done(((f32[512,8]{1,0:T(8,128)}), f32[16,8]{1,0:T(8,128)}) %reduce-scatter.22.cloned.1.call-update) | async-done | bytes 528
  697.5 2.5 fusion.31
  700.0 37.1 %all-reduce.17 = (f32[512]{0:T(512)S(1)}, f32[512]{0:T(512)S(1)}, f32[512]{0:T(512)S(1)}, f32[512]{0:T(512)S(1)}) all-reduce(f32[512]{0:T(512)S(1)} %get-tuple-element.13, f32[512]{0:T(512)S(1)} %get-tuple-element.18, f32[512]{0:T(512)S(1)} %get-tuple-element.11, ...), channel_id=8, replica_groups=mesh['fsdp'=2,'ctx'=4,'tp'=4] {'fsdp','ctx','tp'}, use_global_device_ids=true, to_apply=%region_31.32.clone | all-reduce | flops 2048 | bytes 16384
  740.5 91.7 %reduce-scatter.16.cloned.1.call-done = f32[16,512]{1,0:T(8,128)} async-done(((f32[512,512]{1,0:T(8,128)}), f32[16,512]{1,0:T(8,128)}) %reduce-scatter.16.cloned.1.call-update) | async-done | bytes 32784 | tf_op jit(solution)/shard_map/reduce_scatter | solution.py:280
  832.3 105.1 %reduce-scatter.14.cloned.1.call-done = f32[16,1536]{1,0:T(8,128)} async-done(((f32[512,1536]{1,0:T(8,128)}), f32[16,1536]{1,0:T(8,128)}) %reduce-scatter.14.cloned.1.call-update) | async-done | bytes 98320 | tf_op jit(solution)/shard_map/reduce_scatter | solution.py:279
  937.3 74.3 %reduce-scatter.20.cloned.1.call-done = f32[8,64,512]{2,1,0:T(8,128)} async-done(((f32[8,512,512]{2,1,0:T(8,128)}), f32[8,64,512]{2,1,0:T(8,128)}) %reduce-scatter.20.cloned.1.call-update) | async-done | bytes 1048592 | tf_op jit(solution)/shard_map/reduce_scatter | solution.py:289
  1011.6 75.3 %reduce-scatter.18.cloned.1.call-done = f32[8,64,512]{2,1,0:T(8,128)} async-done(((f32[8,512,512]{2,1,0:T(8,128)}), f32[8,64,512]{2,1,0:T(8,128)}) %reduce-scatter.18.cloned.1.call-update) | async-done | bytes 1048592 | tf_op jit(solution)/shard_map/reduce_scatter | solution.py:288
  (283 shorter events, 75.9 us)
Async XLA Ops:
  8.0 63.4 %all-gather.9.cloned.1.call-start = ((), (), s32[]{:S(2)}) async-start(), calls=%async_computation.9 | async-start | bytes 1622016 | tf_op jit(solution)/shard_map/all_gather | solution.py:112
  11.0 60.5 %copy-start.26 = (bf16[16,512]{1,0:T(8,128)(2,1)}, bf16[16,512]{1,0:T(8,128)(2,1)S(1)}, u32[]{:S(2)}) copy-start(bf16[16,512]{1,0:T(8,128)(2,1)S(1)} %get-tuple-element.37) | copy-start | bytes 49156
  11.0 49.4 %collective-permute-start = (bf16[16,512]{1,0:T(8,128)(2,1)S(1)}, bf16[16,512]{1,0:T(8,128)(2,1)S(1)}, u32[]{:S(2)}, u32[]{:S(2)}) collective-permute-start(bf16[16,512]{1,0:T(8,128)(2,1)S(1)} %get-tuple-element.37), channel_id=1, source_target_pairs={{0,31},{1,0},{2,1},{3,2},{4,3},{5,4},{6,5},{7,6},{8,7},{9,8},{10,9... | collective-permute-start | bytes 49160 | tf_op jit(solution)/shard_map/ppermute | solution.py:22
  18.5 52.9 %copy-start.41 = (f32[394]{0:T(512)}, f32[394]{0:T(512)S(1)}, u32[]{:S(2)}) copy-start(f32[394]{0:T(512)S(1)} %broadcast_multiply_fusion.6) | copy-start | bytes 4732
  19.8 51.6 %copy-start.46 = (f32[394]{0:T(512)}, f32[394]{0:T(512)S(1)}, u32[]{:S(2)}) copy-start(f32[394]{0:T(512)S(1)} %add_rsqrt_fusion.1) | copy-start | bytes 4732
  60.4 11.1 %copy-start.48 = (f32[512]{0:T(512)}, f32[512]{0:T(512)S(1)}, u32[]{:S(2)}) copy-start(f32[512]{0:T(512)S(1)} %convert_element_type.128) | copy-start | bytes 6148
  60.4 11.1 %copy-start.52 = (f32[512]{0:T(512)}, f32[512]{0:T(512)S(1)}, u32[]{:S(2)}) copy-start(f32[512]{0:T(512)S(1)} %convert_element_type.130) | copy-start | bytes 6148
  60.4 11.1 %copy-start.32 = (bf16[16,512]{1,0:T(8,128)(2,1)}, bf16[16,512]{1,0:T(8,128)(2,1)S(1)}, u32[]{:S(2)}) copy-start(bf16[16,512]{1,0:T(8,128)(2,1)S(1)} %collective-permute-done) | copy-start | bytes 49156
  60.4 5.6 collective-permute-start.1
  66.1 2.5 collective-permute-start.2
  68.5 11.5 %copy-start.25 = (bf16[64,512]{1,0:T(8,128)(2,1)}, bf16[64,512]{1,0:T(8,128)(2,1)S(1)}, u32[]{:S(2)}) copy-start(bf16[64,512]{1,0:T(8,128)(2,1)S(1)} %collective-permute-done.2) | copy-start | bytes 196612
  69.2 10.8 collective-permute-start.3
  74.4 7.6 copy-start.55
  74.4 8.2 copy-start.54
  74.4 15.4 %copy-start.27 = (bf16[16,512]{1,0:T(8,128)(2,1)S(1)}, bf16[16,512]{1,0:T(8,128)(2,1)}, u32[]{:S(2)}) copy-start(bf16[16,512]{1,0:T(8,128)(2,1)} %copy-done.26) | copy-start | bytes 49156
  74.4 15.4 %copy-start.33 = (bf16[16,512]{1,0:T(8,128)(2,1)S(1)}, bf16[16,512]{1,0:T(8,128)(2,1)}, u32[]{:S(2)}) copy-start(bf16[16,512]{1,0:T(8,128)(2,1)} %copy-done.32) | copy-start | bytes 49156
  74.4 15.4 %copy-start.29 = (bf16[32,512]{1,0:T(8,128)(2,1)S(1)}, bf16[32,512]{1,0:T(8,128)(2,1)}, u32[]{:S(2)}) copy-start(bf16[32,512]{1,0:T(8,128)(2,1)} %copy-done.28) | copy-start | bytes 98308
  76.4 19.7 %all-to-all-start = ((bf16[2,197,3,4,128]{4,0,2,1,3:T(2,128)(2,1)}), bf16[2,197,3,4,128]{4,0,2,1,3:T(2,128)(2,1)S(1)}, u32[]{:S(2)}, u32[]{:S(2)}) async-start(bf16[2,197,3,4,128]{4,0,2,1,3:T(2,128)(2,1)} %copy.128), calls=%async_computation | async-start | bytes 2420736 | tf_op jit(solution)/shard_map/all_to_all | solution.py:132
  79.9 157.2 %all-gather.17.cloned.1.call-start = ((), (), s32[]{:S(2)}) async-start(), calls=%async_computation.17 | async-start | bytes 2048000 | tf_op jit(solution)/shard_map/all_gather | solution.py:160
  81.0 8.8 collective-permute-start.4
  89.8 9.3 copy-start.23
  89.9 9.3 copy-start.19
  104.0 11.9 %copy-start.24 = (bf16[256,512]{1,0:T(8,128)(2,1)S(1)}, bf16[256,512]{1,0:T(8,128)(2,1)}, u32[]{:S(2)}) copy-start(bf16[256,512]{1,0:T(8,128)(2,1)} %copy-done.23) | copy-start | bytes 786436
  107.2 16.8 %copy-start.37 = (f32[512]{0:T(512)S(1)}, f32[512]{0:T(512)}, u32[]{:S(2)}) copy-start(f32[512]{0:T(512)} %convert_element_type.139) | copy-start | bytes 6148
  107.2 16.8 %copy-start.44 = (f32[512]{0:T(512)S(1)}, f32[512]{0:T(512)}, u32[]{:S(2)}) copy-start(f32[512]{0:T(512)} %convert_element_type.141) | copy-start | bytes 6148
  109.2 11.0 %all-to-all-start.1 = ((bf16[8,197,1,128]{3,1,2,0:T(8,128)(2,1)}), bf16[8,197,1,128]{3,1,2,0:T(8,128)(2,1)S(1)}, u32[]{:S(2)}, u32[]{:S(2)}) async-start(bf16[8,197,1,128]{3,1,2,0:T(8,128)(2,1)} %copy.134), calls=%async_computation.1 | async-start | bytes 819200 | tf_op jit(solution)/shard_map/all_to_all | solution.py:147
  112.7 12.3 %copy-start.21 = (f32[8,64,512]{2,1,0:T(8,128)S(1)}, f32[8,64,512]{2,1,0:T(8,128)}, u32[]{:S(2)}) copy-start(f32[8,64,512]{2,1,0:T(8,128)} %param.21) | copy-start | bytes 3145732
  112.7 147.5 %all-gather.15.cloned.1.call-start = ((), (), s32[]{:S(2)}) async-start(), calls=%async_computation.16 | async-start | bytes 2048000 | tf_op jit(solution)/shard_map/all_gather | solution.py:159
  121.4 75.3 %copy-start.34 = (s32[1576,2]{0,1:T(2,128)S(1)}, s32[1576,2]{0,1:T(2,128)}, u32[]{:S(2)}) copy-start(s32[1576,2]{0,1:T(2,128)} %param.23) | copy-start | bytes 37828
  123.1 73.9 %copy-start.50 = (s32[1,1576]{1,0:T(1,128)S(1)}, s32[1,1576]{1,0:T(1,128)}, u32[]{:S(2)}) copy-start(s32[1,1576]{1,0:T(1,128)} %param.24) | copy-start | bytes 18916
  123.1 86.2 %copy-start.35 = (f32[394]{0:T(512)}, f32[394]{0:T(512)S(1)}, u32[]{:S(2)}) copy-start(f32[394]{0:T(512)S(1)} %broadcast_multiply_fusion.5) | copy-start | bytes 4732
  124.0 73.0 %copy-start.39 = (f32[394]{0:T(512)}, f32[394]{0:T(512)S(1)}, u32[]{:S(2)}) copy-start(f32[394]{0:T(512)S(1)} %add_rsqrt_fusion) | copy-start | bytes 4732
  125.0 156.3 %all-gather.11.cloned.1.call-start = ((), (), s32[]{:S(2)}) async-start(), calls=%async_computation.10 | async-start | bytes 4718592 | tf_op jit(solution)/shard_map/all_gather | solution.py:81
  125.9 164.3 %all-gather.13.cloned.1.call-start = ((), (), s32[]{:S(2)}) async-start(), calls=%async_computation.11 | async-start | bytes 4718592 | tf_op jit(solution)/shard_map/all_gather | solution.py:82
  216.7 18.5 %copy-start.57 = (u32[32]{0:T(128)S(1)}, u32[32]{0:T(128)}, u32[]{:S(2)}) copy-start(u32[32]{0:T(128)} %constant.134) | copy-start | bytes 388
  219.4 32.2 %copy-start.43 = (s32[3152]{0:T(1024)}, s32[3152]{0:T(1024)S(1)}, u32[]{:S(2)}) copy-start(s32[3152]{0:T(1024)S(1)} %fusion.44) | copy-start | bytes 37828
  321.9 8.5 copy-start.13
  330.4 20.8 %copy-start.14 = (f32[1576,2]{1,0:T(8,128)S(1)}, f32[1576,2]{1,0:T(8,128)}, u32[]{:S(2)}) copy-start(f32[1576,2]{1,0:T(8,128)} %copy.143) | copy-start | bytes 37828
  367.9 13.9 %copy-start.2 = (bf16[8,512,512]{2,1,0:T(8,128)(2,1)S(1)}, bf16[8,512,512]{2,1,0:T(8,128)(2,1)}, u32[]{:S(2)}) copy-start(bf16[8,512,512]{2,1,0:T(8,128)(2,1)} %all-gather.11.cloned.1.call-done) | copy-start | bytes 12582916
  464.9 77.5 %collective-permute-start.5 = (bf16[18,512]{1,0:T(8,128)(2,1)S(1)}, bf16[18,512]{1,0:T(8,128)(2,1)}, u32[]{:S(2)}, u32[]{:S(2)}) collective-permute-start(bf16[18,512]{1,0:T(8,128)(2,1)S(1)} %slice.41), channel_id=1, source_target_pairs={{0,1},{1,2},{2,3},{4,5},{5,6},{6,7},{8,9},{9,10},{10,11},{12,13},{... | collective-permute-start | bytes 55304
  467.4 74.9 %copy-start.16 = (bf16[400,512]{1,0:T(8,128)(2,1)S(1)}, bf16[400,512]{1,0:T(8,128)(2,1)}, u32[]{:S(2)}) copy-start(bf16[400,512]{1,0:T(8,128)(2,1)} %copy-done.15) | copy-start | bytes 1228804
  467.4 78.8 %copy-start.4 = (f32[394,512]{1,0:T(8,128)S(1)}, f32[394,512]{1,0:T(8,128)}, u32[]{:S(2)}) copy-start(f32[394,512]{1,0:T(8,128)} %copy-done.3) | copy-start | bytes 2420740
  467.4 78.9 %copy-start.36 = (f32[394]{0:T(512)S(1)}, f32[394]{0:T(512)}, u32[]{:S(2)}) copy-start(f32[394]{0:T(512)} %copy-done.35) | copy-start | bytes 4732
  467.4 78.9 %copy-start.38 = (f32[512]{0:T(512)S(1)}, f32[512]{0:T(512)}, u32[]{:S(2)}) copy-start(f32[512]{0:T(512)} %convert_element_type.139) | copy-start | bytes 6148
  467.4 78.9 %copy-start.40 = (f32[394]{0:T(512)S(1)}, f32[394]{0:T(512)}, u32[]{:S(2)}) copy-start(f32[394]{0:T(512)} %copy-done.39) | copy-start | bytes 4732
  535.2 11.9 %copy-start.17 = (bf16[394,512]{1,0:T(8,128)(2,1)S(1)}, bf16[394,512]{1,0:T(8,128)(2,1)}, u32[]{:S(2)}) copy-start(bf16[394,512]{1,0:T(8,128)(2,1)} %param.25) | copy-start | bytes 1210372
  535.2 5.3 collective-permute-start.7
  537.6 6.7 collective-permute-start.6
  547.0 11.5 %copy-start.45 = (f32[512]{0:T(512)S(1)}, f32[512]{0:T(512)}, u32[]{:S(2)}) copy-start(f32[512]{0:T(512)} %convert_element_type.141) | copy-start | bytes 6148
  550.3 17.8 %copy-start.1 = (f32[8,2,197,197]{2,3,1,0:T(8,128)S(1)}, f32[8,2,197,197]{2,3,1,0:T(8,128)}, u32[]{:S(2)}) copy-start(f32[8,2,197,197]{2,3,1,0:T(8,128)} %copy-done) | copy-start | bytes 7451332
  550.3 17.8 %copy-start.31 = (f32[2,8,197]{2,1,0:T(8,128)S(1)}, f32[2,8,197]{2,1,0:T(8,128)}, u32[]{:S(2)}) copy-start(f32[2,8,197]{2,1,0:T(8,128)} %copy-done.30) | copy-start | bytes 37828
  554.4 11.7 %all-to-all-start.2 = ((bf16[2,197,4,128]{3,0,1,2:T(2,128)(2,1)}), bf16[2,197,4,128]{3,0,1,2:T(2,128)(2,1)}, u32[]{:S(2)}, u32[]{:S(2)}) async-start(bf16[2,197,4,128]{3,0,1,2:T(2,128)(2,1)} %copy.145), calls=%async_computation.2 | async-start | bytes 806912 | tf_op jit(solution)/shard_map/all_to_all | solution.py:234
  558.5 137.6 %reduce-scatter.22.cloned.1.call-start = ((), (), s32[]{:S(2)}) async-start(), calls=%async_computation.18 | async-start | bytes 270336
  560.9 271.4 %reduce-scatter.16.cloned.1.call-start = ((), (), s32[]{:S(2)}) async-start(), calls=%async_computation.13 | async-start | bytes 1081344 | tf_op jit(solution)/shard_map/reduce_scatter | solution.py:280
  563.7 373.6 %reduce-scatter.14.cloned.1.call-start = ((), (), s32[]{:S(2)}) async-start(), calls=%async_computation.12 | async-start | bytes 3244032 | tf_op jit(solution)/shard_map/reduce_scatter | solution.py:279
  585.7 21.1 %copy-start.10 = (bf16[394,512]{1,0:T(8,128)(2,1)S(1)}, bf16[394,512]{1,0:T(8,128)(2,1)}, u32[]{:S(2)}) copy-start(bf16[394,512]{1,0:T(8,128)(2,1)} %param.13) | copy-start | bytes 1210372
  585.7 21.1 %copy-start.42 = (f32[394]{0:T(512)S(1)}, f32[394]{0:T(512)}, u32[]{:S(2)}) copy-start(f32[394]{0:T(512)} %copy-done.41) | copy-start | bytes 4732
  585.7 21.1 %copy-start.47 = (f32[394]{0:T(512)S(1)}, f32[394]{0:T(512)}, u32[]{:S(2)}) copy-start(f32[394]{0:T(512)} %copy-done.46) | copy-start | bytes 4732
  585.7 21.1 %copy-start.49 = (f32[512]{0:T(512)S(1)}, f32[512]{0:T(512)}, u32[]{:S(2)}) copy-start(f32[512]{0:T(512)} %copy-done.48) | copy-start | bytes 6148
  585.7 21.1 %copy-start.53 = (f32[512]{0:T(512)S(1)}, f32[512]{0:T(512)}, u32[]{:S(2)}) copy-start(f32[512]{0:T(512)} %copy-done.52) | copy-start | bytes 6148
  610.9 400.7 %reduce-scatter.20.cloned.1.call-start = ((), (), s32[]{:S(2)}) async-start(), calls=%async_computation.15 | async-start | bytes 9437184 | tf_op jit(solution)/shard_map/reduce_scatter | solution.py:289
  624.8 462.1 %reduce-scatter.18.cloned.1.call-start = ((), (), s32[]{:S(2)}) async-start(), calls=%async_computation.14 | async-start | bytes 9437184 | tf_op jit(solution)/shard_map/reduce_scatter | solution.py:288
  634.1 63.4 %copy-start.18 = (bf16[394,1536]{1,0:T(8,128)(2,1)S(1)}, bf16[394,1536]{1,0:T(8,128)(2,1)}, u32[]{:S(2)}) copy-start(bf16[394,1536]{1,0:T(8,128)(2,1)} %reshape.267) | copy-start | bytes 3631108
  634.1 105.3 %copy-start.8 = (f32[394,512]{1,0:T(8,128)S(1)}, f32[394,512]{1,0:T(8,128)}, u32[]{:S(2)}) copy-start(f32[394,512]{1,0:T(8,128)} %copy-done.7) | copy-start | bytes 2420740
  (15 other events, 48.2 us)
Sparse Core Ops, SparseCore 0:
  12.3 57.8 all-gather.8
  561.5 134.5 reduce-scatter.21
  698.9 133.2 reduce-scatter.15
  838.1 99.1 reduce-scatter.13
  941.2 70.3 reduce-scatter.19
  1015.5 71.3 reduce-scatter.17
Sparse Core Ops, SparseCore 1:
  82.1 39.9 all-gather.16
  125.1 38.8 all-gather.14
  165.7 35.4 all-gather.10
  203.0 36.5 all-gather.12
